TPU v7x, 512 devices: a whole 4x8x8 slice. The times are simulated.
512 devices in a mesh: doc: 32 (over z, x), cent: 16 (over y, core).
Axes of the slice: x: 4, y: 8, z: 8, core: 2. Of those that a mesh axis runs over, the one named last changes fastest.
Arguments:
- rows: bfloat16 [65536, 1024], P('doc'), may hold values from -30 to 30
- centroids: bfloat16 [8192, 1024], P('cent'), may hold values from -16 to 16
Outputs:
- new_centroids: float32 [8192, 1024], P(('cent', 'doc'))
All inputs are finite; a program needn't handle non-finite values.
Results may differ from a plain program's by a relative error of at most 0.0009.
Values sent between devices are 32-bit elements; how exact they have to be, the bound alone decides.
A program may use at most 64 MiB of HBM per device.

v0:
```python
import math

import jax
import jax.numpy as jnp
from jax import lax
from jax.sharding import PartitionSpec as P


def on_device(rows, centroids):
    scale = 1.0 / (0.6 * math.sqrt(rows.shape[1]))
    logits = jnp.einsum("rd,kd->rk", rows, centroids, preferred_element_type=jnp.float32) * scale
    local_max = jnp.max(logits, axis=1)
    highest = lax.pmax(local_max, "cent")
    total = lax.psum(jnp.sum(jnp.exp(logits - highest[:, None]), axis=1), "cent")
    lse = highest + jnp.log(total)
    resp = jnp.exp(logits - lse[:, None]).astype(jnp.bfloat16)
    sums = jnp.einsum("rk,rd->kd", resp, rows, preferred_element_type=jnp.float32)
    totals = jnp.sum(resp, axis=0, dtype=jnp.float32)
    share = centroids.shape[0] // lax.axis_size("doc")
    start = lax.axis_index("doc") * share
    own_rows = lax.dynamic_slice_in_dim(centroids, start, share, 0).astype(jnp.float32)
    whole_sums, whole_totals = lax.psum((sums, totals), "doc")
    part_sums = lax.dynamic_slice_in_dim(whole_sums, start, share, 0)
    part_totals = lax.dynamic_slice_in_dim(whole_totals, start, share, 0)
    return (part_sums + own_rows) / (part_totals[:, None] + 1.0)


def solution(mesh):
    return jax.shard_map(
        on_device,
        mesh=mesh,
        in_specs=(P("doc", None), P("cent", None)),
        out_specs=P(("cent", "doc"), None),
        check_vma=False,
    )
```

profile of v0, /device:TPU:1, one launch (start us, length us, event | category | flops | bytes accessed | tf_op | source)
XLA Modules:
  0.0 247.2 jit_solution(16175770408922332020)
XLA Ops:
  6.5 0.0 all-reduce.2.cloned.1.call-start
  6.5 6.8 %multiply_reduce_fusion = (f32[2048]{0:T(1024)S(1)}, f32[2048,512]{0,1:T(8,128)}) fusion(bf16[2048,1024]{1,0:T(8,128)(2,1)} %param.2, bf16[512,1024]{1,0:T(8,128)(2,1)} %param.3), kind=kOutput, calls=%fused_computation.3 | convolution fusion | flops 2149578752 | bytes 9445376 | tf_op jit(solution)/shard_map/rd,kd->rk/dot_general | solution.py:11
  13.3 30.2 %pmax.7 = f32[2048]{0:T(1024)S(1)} all-reduce(f32[2048]{0:T(1024)S(1)} %get-tuple-element.5), channel_id=1, replica_groups=mesh['doc'=32,'cent'=16] {'cent'}, use_global_device_ids=true, to_apply=%region_1.0 | all-reduce | flops 2048 | bytes 16384 | tf_op jit(solution)/shard_map/pmax | solution.py:13
  43.5 2.9 %exponential_reduce_fusion = f32[2048]{0:T(1024)S(1)} fusion(f32[2048,512]{0,1:T(8,128)} %get-tuple-element.6, f32[2048]{0:T(1024)S(1)} %pmax.7), kind=kLoop, calls=%fused_computation.2 | loop fusion | flops 3143680 | bytes 4210688 | tf_op jit(solution)/shard_map/reduce_sum | solution.py:14
  46.4 24.0 %psum.21 = f32[2048]{0:T(1024)S(1)} all-reduce(f32[2048]{0:T(1024)S(1)} %exponential_reduce_fusion), channel_id=1, replica_groups=mesh['doc'=32,'cent'=16] {'cent'}, use_global_device_ids=true, to_apply=%region_3.0 | all-reduce | flops 2048 | bytes 16384 | tf_op jit(solution)/shard_map/psum | solution.py:14
  70.5 7.1 %fusion = f32[512,1024]{1,0:T(8,128)} fusion(bf16[2048,1024]{1,0:T(8,128)(2,1)} %param.2, f32[2048,512]{0,1:T(8,128)} %get-tuple-element.6, f32[2048]{0:T(1024)S(1)} %log_add_fusion), kind=kOutput, calls=%fused_computation.4 | convolution fusion | flops 2150629376 | bytes 10493952 | tf_op jit(solution)/shard_map/rk,rd->kd/dot_general | solution.py:17
  77.7 0.0 all-reduce.2.cloned.1.call-update
  77.7 2.9 %convert_reduce_fusion = f32[512]{0:T(512)S(1)} fusion(f32[2048]{0:T(1024)S(1)} %log_add_fusion, f32[2048,512]{0,1:T(8,128)} %get-tuple-element.6), kind=kLoop, calls=%fused_computation | loop fusion | flops 5242368 | bytes 4204544 | tf_op jit(solution)/shard_map/reduce_sum | solution.py:18
  80.6 64.4 %psum.23 = f32[512]{0:T(512)S(1)} all-reduce(f32[512]{0:T(512)S(1)} %convert_reduce_fusion), channel_id=1, replica_groups=mesh['doc'=32,'cent'=16] {'doc'}, use_global_device_ids=true, to_apply=%region_6.0 | all-reduce | flops 512 | bytes 4096 | tf_op jit(solution)/shard_map/psum | solution.py:22
  145.1 0.1 dynamic-slice_add_fusion
  145.2 93.6 %all-reduce.2.cloned.1.call-done = f32[512,1024]{1,0:T(8,128)} async-done(((f32[512,1024]{1,0:T(8,128)}), f32[512,1024]{1,0:T(8,128)}) %all-reduce.2.cloned.1.call-update) | async-done | bytes 2097168 | tf_op jit(solution)/shard_map/psum | solution.py:22
  238.8 1.5 add_divide_fusion
  (1 shorter events, 0.0 us)
Async XLA Ops:
  6.5 232.3 %all-reduce.2.cloned.1.call-start = ((), (), s32[]{:S(2)}) async-start(), calls=%async_computation | async-start | bytes 4194304 | tf_op jit(solution)/shard_map/psum | solution.py:22
Sparse Core Ops, SparseCore 0:
  77.8 160.9 all-reduce.1
where the time goes:
time: 250 us; the launch traced here: 247 us
  blocking collectives  119 us (48%)
  waiting for transfers between devices  93.7 us (37%)
  matrix products  13.9 us (6%)
  between operations  13.4 us (5%)
  other arithmetic  7.48 us (3%)
    psum x1, waiting for transfers between devices, on_device(): whole_sums, whole_totals = lax.psum((sums, totals), 'doc')  93.6 us
    psum x1, blocking collectives, on_device(): whole_sums, whole_totals = lax.psum((sums, totals), 'doc')  64.4 us
    pmax x1, blocking collectives, on_device(): highest = lax.pmax(local_max, 'cent')  30.2 us
    psum x1, blocking collectives, on_device(): lax.psum(jnp.sum(jnp.exp(logits - highest[:, None]), axis=1), 'cent')  24 us
    dot_general x1, matrix products, on_device(): jnp.einsum('rk,rd->kd', resp, rows, preferred_element_type=jnp.float32)  7.14 us
    dot_general x1, matrix products, on_device(): jnp.einsum('rd,kd->rk', rows, centroids, preferred_element_type=jnp.float32)  6.77 us
  transfers between devices with their start and end apart: 1, of which 1 were waited for; matrix products, arithmetic and copies ran while one was open for 1% of the time, Pallas kernels for 0%

commit v1 on v0

v1 whole, which is shorter than its diff:
```python
import math

import jax
import jax.numpy as jnp
from jax import lax
from jax.sharding import PartitionSpec as P


def on_device(rows, centroids):
    scale = 1.0 / (0.6 * math.sqrt(rows.shape[1]))
    logits = jnp.einsum("kd,rd->kr", centroids, rows, preferred_element_type=jnp.float32) * scale
    top = jnp.max(logits, axis=0)
    part = jnp.sum(jnp.exp(logits - top[None, :]), axis=0)
    stats = lax.all_gather(top + jnp.log(part), "cent")
    highest = jnp.max(stats, axis=0)
    lse = highest + jnp.log(jnp.sum(jnp.exp(stats - highest[None, :]), axis=0))
    resp = jnp.exp(logits - lse[None, :]).astype(jnp.bfloat16)
    sums = jnp.einsum("kr,rd->kd", resp, rows, preferred_element_type=jnp.float32)
    totals = jnp.sum(resp, axis=1, dtype=jnp.float32)
    both = jnp.concatenate([sums, jnp.broadcast_to(totals[:, None], (sums.shape[0], 128))], axis=1)
    mine = lax.psum_scatter(both, "doc", scatter_dimension=0, tiled=True)
    share = mine.shape[0]
    start = lax.axis_index("doc") * share
    own_rows = lax.dynamic_slice_in_dim(centroids, start, share, 0).astype(jnp.float32)
    width = rows.shape[1]
    return (mine[:, :width] + own_rows) / (mine[:, width : width + 1] + 1.0)


def solution(mesh):
    return jax.shard_map(
        on_device,
        mesh=mesh,
        in_specs=(P("doc", None), P("cent", None)),
        out_specs=P(("cent", "doc"), None),
        check_vma=False,
    )
```

time: 250 us -> 276 us (1.10)
  waiting for transfers between devices: 93.7 us -> 219 us
  blocking collectives: 119 us -> 21.2 us
  matrix products: 13.9 us -> 10.8 us
    reduce_scatter x0 -> x1, waiting for transfers between devices: none -> 219 us  [on_device(): mine = lax.psum_scatter(both, 'doc', scatter_dimension=0, tiled=True)]
    psum x1 -> x0, waiting for transfers between devices: 93.6 us -> none  [on_device(): whole_sums, whole_totals = lax.psum((sums, totals), 'doc')]
    psum x2 -> x0, blocking collectives: 88.5 us -> none  [the longest x1 64.4 us: on_device(): whole_sums, whole_totals = lax.psum((sums, totals), 'doc')]
    pmax x1 -> x0, blocking collectives: 30.2 us -> none  [on_device(): highest = lax.pmax(local_max, 'cent')]
    all_gather x0 -> x1, blocking collectives: none -> 21.2 us  [on_device(): stats = lax.all_gather(top + jnp.log(part), 'cent')]
    reduce_sum x2 -> x3, other arithmetic: 5.85 us -> 1.53 us  [the longest x1 0.78 us: on_device(): totals = jnp.sum(resp, axis=1, dtype=jnp.float32)]
    dot_general x2, matrix products: 13.9 us -> 10.8 us  [the longest x1 5.93 us: on_device(): jnp.einsum('kr,rd->kd', resp, rows, preferred_element_type=jnp.float32)]
  transfers between devices with their start and end apart: 1 -> 1, of which waited for: 1 -> 1; matrix products, arithmetic and copies ran while one was open for 1% -> 0% of each run, Pallas kernels for 0% -> 0%
where the time goes in v1:
time: 276 us; the launch traced here: 272 us
  waiting for transfers between devices  219 us (79%)
  blocking collectives  21.2 us (8%)
  between operations  13.5 us (5%)
  matrix products  10.8 us (4%)
  other arithmetic  5.54 us (2%)
    reduce_scatter x1, waiting for transfers between devices, on_device(): mine = lax.psum_scatter(both, 'doc', scatter_dimension=0, tiled=True)  219 us
    all_gather x1, blocking collectives, on_device(): stats = lax.all_gather(top + jnp.log(part), 'cent')  21.2 us
    dot_general x1, matrix products, on_device(): jnp.einsum('kr,rd->kd', resp, rows, preferred_element_type=jnp.float32)  5.93 us
  transfers between devices with their start and end apart: 1, of which 1 were waited for; matrix products, arithmetic and copies ran while one was open for 0% of the time, Pallas kernels for 0%

profile of v1, /device:TPU:1, one launch (start us, length us, event | category | flops | bytes accessed | tf_op | source)
XLA Modules:
  0.0 271.9 jit_solution(4398784320786496380)
XLA Ops:
  6.5 0.0 reduce-scatter.2.cloned.1.call-start
  6.5 4.9 %multiply_reduce_fusion = (f32[2048]{0:T(1024)S(1)}, f32[512,2048]{1,0:T(8,128)S(1)}) fusion(bf16[512,1024]{1,0:T(8,128)(2,1)} %param.3, bf16[2048,1024]{1,0:T(8,128)(2,1)} %param.2), kind=kOutput, calls=%fused_computation.3 | convolution fusion | flops 2149578752 | bytes 9445376 | tf_op jit(solution)/shard_map/kd,rd->kr/dot_general | solution.py:11
  11.4 0.0 copy-start
  11.4 1.9 copy-done
  13.4 0.7 exponential_reduce_fusion
  14.1 21.2 %all-gather = f32[32768]{0:T(1024)S(1)} all-gather(f32[2048]{0:T(1024)S(1)} %log_add_fusion.1), channel_id=2, replica_groups=mesh['doc'=32,'cent'=16] {'cent'}, dimensions={0}, use_global_device_ids=true | all-gather | bytes 139264 | tf_op jit(solution)/shard_map/all_gather | solution.py:14
  35.4 0.0 copy-start.1
  35.4 5.9 %fusion = f32[512,1024]{1,0:T(8,128)S(1)} fusion(bf16[2048,1024]{1,0:T(8,128)(2,1)} %param.2, f32[512,2048]{1,0:T(8,128)} %copy-done, f32[2048]{0:T(1024)S(1)} %log_add_fusion), kind=kOutput, calls=%fused_computation.5 | convolution fusion | flops 2150629376 | bytes 10493952 | tf_op jit(solution)/shard_map/kr,rd->kd/dot_general | solution.py:18
  41.4 0.0 copy-done.1
  41.4 0.8 convert_reduce_fusion
  42.2 0.1 broadcast_in_dim.2
  42.3 1.6 pad_maximum_fusion
  43.9 0.0 reduce-scatter.2.cloned.1.call-update
  43.9 218.8 %reduce-scatter.2.cloned.1.call-done = f32[16,1152]{1,0:T(8,128)} async-done(((f32[512,1152]{1,0:T(8,128)}), f32[16,1152]{1,0:T(8,128)}) %reduce-scatter.2.cloned.1.call-update) | async-done | bytes 73744 | tf_op jit(solution)/shard_map/reduce_scatter | solution.py:21
  262.7 0.8 fusion.2
  263.5 1.6 fusion.1
  (5 shorter events, 0.1 us)
Async XLA Ops:
  6.5 256.2 %reduce-scatter.2.cloned.1.call-start = ((), (), s32[]{:S(2)}) async-start(), calls=%async_computation.1 | async-start | bytes 2433024 | tf_op jit(solution)/shard_map/reduce_scatter | solution.py:21
  11.4 1.9 copy-start
  35.4 5.9 %copy-start.1 = (f32[512,2048]{1,0:T(8,128)S(1)}, f32[512,2048]{1,0:T(8,128)}, u32[]{:S(2)}) copy-start(f32[512,2048]{1,0:T(8,128)} %copy-done) | copy-start | bytes 12582916
Sparse Core Ops, SparseCore 0:
  44.0 218.5 reduce-scatter.1

commit v2 on v0

v2 whole, which is shorter than its diff:
```python
import functools
import math

import jax
import jax.numpy as jnp
from jax import lax
from jax.experimental import pallas as pl
from jax.experimental.pallas import tpu as pltpu
from jax.sharding import PartitionSpec as P

MESH = pl.DeviceIdType.MESH
F32 = jnp.float32
NZ, NX = 8, 4
LANES = 128
BLOCKS = ((0, 256, True), (256, 256, False), (512, 256, True), (768, 256, False))


def ring(me, n, device, data, half_in, full_in, send_sems, recv_sems, sent):
    h = data.shape[1] // 2
    last = n // 2
    copies = [None, None]
    for step in range(1, last + 1):
        for way, sign in enumerate((1, -1)):
            chunk = data.at[lax.rem(me + sign * (last + 1 - step) + n, n)]
            half = pl.ds(way * h, h)
            if step == 1:
                source, target = chunk.at[half], half_in.at[way]
            else:
                copies[way].wait_recv()
                if step == 2:
                    chunk[half] += half_in[way]
                else:
                    chunk[...] += full_in[way, step - 3]
                source, target = chunk, full_in.at[way, step - 2]
            copies[way] = pltpu.make_async_remote_copy(
                src_ref=source,
                dst_ref=target,
                send_sem=send_sems.at[way, step - 1],
                recv_sem=recv_sems.at[way, step - 1],
                device_id=device(lax.rem(me + sign + n, n)),
                device_id_type=MESH,
            )
            copies[way].start()
            sent.append(copies[way])
        yield
    own = data.at[me]
    for way in range(2):
        copies[way].wait_recv()
        own[...] += full_in[way, last - 2]


def kernel(scale, ncent, *refs):
    rows_hbm, cent_ref, out_ref, x_v, p_v, resp_v, top_v, stat_v, tot_v = refs[:9]
    in_sems, stat_send, stat_recv = refs[9:12]
    block_refs = [refs[12 + 9 * b : 21 + 9 * b] for b in range(len(BLOCKS))]
    rows, step = x_v.shape[0], 512
    nsteps = rows // step
    doc, cent = lax.axis_index("doc"), lax.axis_index("cent")
    z, x = doc // NX, lax.rem(doc, NX)

    def chunk_in(i):
        part = pl.ds(pl.multiple_of(i * step, step), step)
        return pltpu.make_async_copy(rows_hbm.at[part], x_v.at[part], in_sems.at[i])

    for i in range(nsteps):
        chunk_in(i).start()

    def at_z(k):
        return {"doc": k * NX + x}

    def at_x(k):
        return {"doc": z * NX + k}

    barrier = pltpu.get_barrier_semaphore()
    near = [at_z(lax.rem(z + 1, NZ)), at_z(lax.rem(z + NZ - 1, NZ))]
    near += [at_x(lax.rem(x + 1, NX)), at_x(lax.rem(x + NX - 1, NX))]
    near += [{"cent": lax.rem(cent + k, ncent)} for k in range(1, ncent)]
    for other in near:
        pl.semaphore_signal(barrier, inc=1, device_id=other, device_id_type=MESH)

    def logits_step(i, carry):
        chunk_in(i).wait()
        part = pl.ds(pl.multiple_of(i * step, step), step)
        logits = lax.dot_general(
            cent_ref[...], x_v[part, :], (((1,), (1,)), ((), ())), preferred_element_type=F32
        ) * scale
        top = jnp.max(logits, axis=0, keepdims=True)
        p = jnp.exp(logits - top)
        p_v[:, part] = p
        top_v[:, part] = top
        stat_v[0, :, part] = top + jnp.log(jnp.sum(p, axis=0, keepdims=True))
        return carry

    lax.fori_loop(0, nsteps, logits_step, 0)
    pl.semaphore_wait(barrier, len(near))

    stat_copies = []
    for k in range(1, ncent):
        stat_copies.append(
            pltpu.make_async_remote_copy(
                src_ref=stat_v.at[0],
                dst_ref=stat_v.at[k],
                send_sem=stat_send.at[k],
                recv_sem=stat_recv.at[k],
                device_id={"cent": lax.rem(cent + k, ncent)},
                device_id_type=MESH,
            )
        )
        stat_copies[-1].start()
    for copy in stat_copies:
        copy.wait_recv()

    stats = stat_v[...]
    highest = jnp.max(stats, axis=0)
    lse = highest + jnp.log(jnp.sum(jnp.exp(stats - highest[None]), axis=0))
    top_v[...] = jnp.exp(top_v[...] - lse)
    tot_v[...] = jnp.zeros_like(tot_v)

    def resp_step(i, carry):
        part = pl.ds(pl.multiple_of(i * step, step), step)
        resp = (p_v[:, part] * top_v[:, part]).astype(jnp.bfloat16)
        resp_v[:, part] = resp
        wide = resp.astype(F32)
        total = tot_v[...]
        for j in range(step // LANES):
            total += wide[:, j * LANES : (j + 1) * LANES]
        tot_v[...] = total
        return carry

    lax.fori_loop(0, nsteps, resp_step, 0)

    sent = []
    active = []
    share = out_ref.shape[0]

    def run(b):
        _, _, x_first = BLOCKS[b]
        data, h1, f1, s1, r1, h2, f2, s2, r2 = block_refs[b]
        first = (x, NX, at_x) if x_first else (z, NZ, at_z)
        second = (z, NZ, at_z) if x_first else (x, NX, at_x)
        yield from ring(*first, data, h1, f1, s1, r1, sent)
        yield from ring(*second, data.at[first[0]], h2, f2, s2, r2, sent)

    def put(data, x_first, first, width, value):
        for k in range(NZ):
            tile = value[k * NX * share : (k + 1) * NX * share].reshape(NX, share, width)
            if x_first:
                data[:, k, :, first : first + width] = tile
            else:
                data[k, :, :, first : first + width] = tile

    for b, (start, width, x_first) in enumerate(BLOCKS):
        data = block_refs[b][0]
        value = jnp.dot(resp_v[...], x_v[:, start : start + width], preferred_element_type=F32)
        put(data, x_first, 0, width, value)
        if b == 0:
            put(data, x_first, width, LANES, tot_v[...])
        active.append(run(b))
        next(active[-1])
    while active:
        for gen in list(active):
            if next(gen, None) is None and gen.gi_frame is None:
                active.remove(gen)

    own = cent_ref[pl.ds(pl.multiple_of(doc * share, share), share), :].astype(F32)
    total = None
    for b, (start, width, x_first) in enumerate(BLOCKS):
        value = block_refs[b][0][(x, z) if x_first else (z, x)]
        if b == 0:
            total = jnp.sum(value[:, width:], axis=1, keepdims=True) + 1.0
        out_ref[:, start : start + width] = (value[:, :width] + own[:, start : start + width]) / total
    for copy in stat_copies + sent:
        copy.wait_send()


def on_device(rows, centroids):
    nrows, d = rows.shape
    local = centroids.shape[0]
    ncent = lax.axis_size("cent")
    share = local // (NZ * NX)
    scale = 1.0 / (0.6 * math.sqrt(d))
    dma = pltpu.SemaphoreType.DMA
    scratch = [
        pltpu.VMEM((nrows, d), jnp.bfloat16),
        pltpu.VMEM((local, nrows), F32),
        pltpu.VMEM((local, nrows), jnp.bfloat16),
        pltpu.VMEM((1, nrows), F32),
        pltpu.VMEM((ncent, 1, nrows), F32),
        pltpu.VMEM((local, LANES), F32),
        dma((nrows // 512,)),
        dma((ncent,)),
        dma((ncent,)),
    ]
    for b, (_, width, x_first) in enumerate(BLOCKS):
        w = width + (LANES if b == 0 else 0)
        n1, n2 = (NX, NZ) if x_first else (NZ, NX)
        scratch += [
            pltpu.VMEM((n1, n2, share, w), F32),
            pltpu.VMEM((2, n2 // 2, share, w), F32),
            pltpu.VMEM((2, n1 // 2 - 1, n2, share, w), F32),
            dma((2, n1 // 2)),
            dma((2, n1 // 2)),
            pltpu.VMEM((2, share // 2, w), F32),
            pltpu.VMEM((2, n2 // 2 - 1, share, w), F32),
            dma((2, n2 // 2)),
            dma((2, n2 // 2)),
        ]
    return pl.pallas_call(
        functools.partial(kernel, scale, ncent),
        out_shape=jax.ShapeDtypeStruct((share, d), F32),
        in_specs=[pl.BlockSpec(memory_space=pl.ANY), pl.BlockSpec(memory_space=pltpu.VMEM)],
        out_specs=pl.BlockSpec(memory_space=pltpu.VMEM),
        scratch_shapes=scratch,
        compiler_params=pltpu.CompilerParams(collective_id=0, has_side_effects=True),
    )(rows, centroids)


def solution(mesh):
    return jax.shard_map(
        on_device,
        mesh=mesh,
        in_specs=(P("doc", None), P("cent", None)),
        out_specs=P(("cent", "doc"), None),
        check_vma=False,
    )
```

time: 250 us -> 58 us (0.23)
  the two profiles are of different devices: /device:TPU:1 before, /device:TPU:2 now
where the time goes in v2:
time: 58 us; the launch traced here: 57.8 us
  Pallas kernels  56.3 us (97%)
  local copies, waits for them, and re-layouts  1.47 us (3%)
    pallas_call x1, Pallas kernels, on_device(): pl.pallas_call(functools.partial(kernel, scale, ncent), out_shape=jax.Sha...  56.3 us
    unnamed x1, local copies, waits for them, and re-layouts  1.47 us

profile of v2, /device:TPU:2, one launch (start us, length us, event | category | flops | bytes accessed | tf_op | source)
XLA Modules:
  0.0 57.8 jit_solution(11296760923577713839)
XLA Ops:
  0.0 56.3 %shard_map.28 = f32[16,1024]{1,0:T(8,128)} custom-call(bf16[2048,1024]{1,0:T(8,128)(2,1)} %refs_0_.1, bf16[512,1024]{1,0:T(8,128)(2,1)} %refs_1_.1), custom_call_target="tpu_custom_call" | custom-call | tf_op jit(solution)/shard_map/pallas_call | solution.py:208
  56.3 1.5 %copy.4 = f32[16,1024]{1,0:T(8,128)} copy(f32[16,1024]{1,0:T(8,128)} %shard_map.28) | data formatting | bytes 131072

commit v3 on v2

--- a/solution.py
+++ b/solution.py
@@ -12,47 +12,84 @@
 F32 = jnp.float32
 NZ, NX = 8, 4
 LANES = 128
-BLOCKS = ((0, 256, True), (256, 256, False), (512, 256, True), (768, 256, False))
-
-
-def ring(me, n, device, data, half_in, full_in, send_sems, recv_sems, sent):
+BLOCKS = ((0, 128, True), (128, 256, False), (384, 256, True), (640, 128, True), (768, 256, False))
+ORDER = (1, 0, 4, 2, 3, 1, 4, 0, 1, 2, 4, 3, 0, 1, 2, 4, 3, 1, 0, 2, 4, 3)
+
+
+def scatter(mode, me, n, device, data, half_in, full_in, send_sems, recv_sems, sent):
     h = data.shape[1] // 2
     last = n // 2
-    copies = [None, None]
-    for step in range(1, last + 1):
-        for way, sign in enumerate((1, -1)):
-            chunk = data.at[lax.rem(me + sign * (last + 1 - step) + n, n)]
-            half = pl.ds(way * h, h)
-            if step == 1:
-                source, target = chunk.at[half], half_in.at[way]
-            else:
-                copies[way].wait_recv()
-                if step == 2:
-                    chunk[half] += half_in[way]
+
+    def chunk_at(way, k):
+        return data.at[lax.rem(me + (k if way == 0 else n - k), n)]
+
+    def send(way, slot, source, k):
+        copy = pltpu.make_async_remote_copy(
+            src_ref=source,
+            dst_ref=half_in.at[way] if slot == 0 else full_in.at[way, slot - 1],
+            send_sem=send_sems.at[way, slot],
+            recv_sem=recv_sems.at[way, slot],
+            device_id=device(lax.rem(me + (k if way == 0 else n - k), n)),
+            device_id_type=MESH,
+        )
+        copy.start()
+        sent.append(copy)
+        return copy
+
+    halves = [pl.ds(0, h), pl.ds(h, h)]
+    both = (0, 1)
+    own = data.at[me]
+    if mode == "direct":
+        far = [send(w, 0, chunk_at(w, last).at[halves[w]], last) for w in both]
+        near = [send(w, 1, chunk_at(w, 1), 1) for w in both]
+        yield
+        for w in both:
+            near[w].wait_recv()
+            far[w].wait_recv()
+        own[...] += full_in[0, 0] + full_in[1, 0]
+        for w in both:
+            own[halves[w]] += half_in[w]
+    elif mode == "hub":
+        far = [send(w, 0, chunk_at(w, 4).at[halves[w]], 2) for w in both]
+        near = [send(w, 1, chunk_at(w, 3), 1) for w in both]
+        yield
+        for w in both:
+            near[w].wait_recv()
+            far[w].wait_recv()
+            hub = chunk_at(w, 2)
+            hub[...] += full_in[w, 0]
+            hub[halves[w]] += half_in[w]
+            far[w] = send(w, 2, hub, 2)
+        near = [send(w, 3, chunk_at(w, 1), 1) for w in both]
+        yield
+        for w in both:
+            near[w].wait_recv()
+            far[w].wait_recv()
+        own[...] += (full_in[0, 1] + full_in[0, 2]) + (full_in[1, 1] + full_in[1, 2])
+    else:
+        copies = [None, None]
+        for slot in range(last):
+            for w in both:
+                chunk = chunk_at(w, last - slot)
+                if slot == 0:
+                    copies[w] = send(w, 0, chunk.at[halves[w]], 1)
+                    continue
+                copies[w].wait_recv()
+                if slot == 1:
+                    chunk[halves[w]] += half_in[w]
                 else:
-                    chunk[...] += full_in[way, step - 3]
-                source, target = chunk, full_in.at[way, step - 2]
-            copies[way] = pltpu.make_async_remote_copy(
-                src_ref=source,
-                dst_ref=target,
-                send_sem=send_sems.at[way, step - 1],
-                recv_sem=recv_sems.at[way, step - 1],
-                device_id=device(lax.rem(me + sign + n, n)),
-                device_id_type=MESH,
-            )
-            copies[way].start()
-            sent.append(copies[way])
-        yield
-    own = data.at[me]
-    for way in range(2):
-        copies[way].wait_recv()
-        own[...] += full_in[way, last - 2]
+                    chunk[...] += full_in[w, slot - 2]
+                copies[w] = send(w, slot, chunk, 1)
+            yield
+        for w in both:
+            copies[w].wait_recv()
+        own[...] += full_in[0, last - 2] + full_in[1, last - 2]
 
 
 def kernel(scale, ncent, *refs):
-    rows_hbm, cent_ref, out_ref, x_v, p_v, resp_v, top_v, stat_v, tot_v = refs[:9]
-    in_sems, stat_send, stat_recv = refs[9:12]
-    block_refs = [refs[12 + 9 * b : 21 + 9 * b] for b in range(len(BLOCKS))]
+    rows_hbm, cent_ref, out_ref, x_v, p_v, resp_v, top_v, stat_v, pair_v, tot_v = refs[:10]
+    in_sems, stat_send, stat_recv = refs[10:13]
+    block_refs = [refs[13 + 9 * b : 22 + 9 * b] for b in range(len(BLOCKS))]
     rows, step = x_v.shape[0], 512
     nsteps = rows // step
     doc, cent = lax.axis_index("doc"), lax.axis_index("cent")
@@ -72,9 +109,11 @@
         return {"doc": z * NX + k}
 
     barrier = pltpu.get_barrier_semaphore()
-    near = [at_z(lax.rem(z + 1, NZ)), at_z(lax.rem(z + NZ - 1, NZ))]
-    near += [at_x(lax.rem(x + 1, NX)), at_x(lax.rem(x + NX - 1, NX))]
-    near += [{"cent": lax.rem(cent + k, ncent)} for k in range(1, ncent)]
+    near = [at_z(lax.rem(z + k, NZ)) for k in (1, 2, NZ - 2, NZ - 1)]
+    near += [at_x(lax.rem(x + k, NX)) for k in range(1, NX)]
+    near += [{"cent": lax.rem(cent + k, ncent)} for k in range(2, ncent, 2)]
+    partner = {"cent": cent + 1 - 2 * lax.rem(cent, 2)}
+    near.append(partner)
     for other in near:
         pl.semaphore_signal(barrier, inc=1, device_id=other, device_id_type=MESH)
 
@@ -94,26 +133,39 @@
     lax.fori_loop(0, nsteps, logits_step, 0)
     pl.semaphore_wait(barrier, len(near))
 
+    def log_sum_exp(values):
+        highest = jnp.max(values, axis=0)
+        return highest + jnp.log(jnp.sum(jnp.exp(values - highest[None]), axis=0))
+
+    chips = ncent // 2
     stat_copies = []
-    for k in range(1, ncent):
+    for k in sorted(range(1, chips), key=lambda k: -min(k, chips - k)):
         stat_copies.append(
             pltpu.make_async_remote_copy(
                 src_ref=stat_v.at[0],
                 dst_ref=stat_v.at[k],
                 send_sem=stat_send.at[k],
                 recv_sem=stat_recv.at[k],
-                device_id={"cent": lax.rem(cent + k, ncent)},
+                device_id={"cent": lax.rem(cent + 2 * k, ncent)},
                 device_id_type=MESH,
             )
         )
         stat_copies[-1].start()
     for copy in stat_copies:
         copy.wait_recv()
-
-    stats = stat_v[...]
-    highest = jnp.max(stats, axis=0)
-    lse = highest + jnp.log(jnp.sum(jnp.exp(stats - highest[None]), axis=0))
-    top_v[...] = jnp.exp(top_v[...] - lse)
+    pair_v[0] = log_sum_exp(stat_v[...])
+    swap = pltpu.make_async_remote_copy(
+        src_ref=pair_v.at[0],
+        dst_ref=pair_v.at[1],
+        send_sem=stat_send.at[0],
+        recv_sem=stat_recv.at[0],
+        device_id=partner,
+        device_id_type=MESH,
+    )
+    swap.start()
+    stat_copies.append(swap)
+    swap.wait_recv()
+    top_v[...] = jnp.exp(top_v[...] - log_sum_exp(pair_v[...]))
     tot_v[...] = jnp.zeros_like(tot_v)
 
     def resp_step(i, carry):
@@ -138,8 +190,9 @@
         data, h1, f1, s1, r1, h2, f2, s2, r2 = block_refs[b]
         first = (x, NX, at_x) if x_first else (z, NZ, at_z)
         second = (z, NZ, at_z) if x_first else (x, NX, at_x)
-        yield from ring(*first, data, h1, f1, s1, r1, sent)
-        yield from ring(*second, data.at[first[0]], h2, f2, s2, r2, sent)
+        yield from scatter("ring", *first, data, h1, f1, s1, r1, sent)
+        mode = "hub" if x_first else "direct"
+        yield from scatter(mode, *second, data.at[first[0]], h2, f2, s2, r2, sent)
 
     def put(data, x_first, first, width, value):
         for k in range(NZ):
@@ -157,10 +210,9 @@
             put(data, x_first, width, LANES, tot_v[...])
         active.append(run(b))
         next(active[-1])
-    while active:
-        for gen in list(active):
-            if next(gen, None) is None and gen.gi_frame is None:
-                active.remove(gen)
+    for b in ORDER:
+        next(active[b], None)
+    assert all(gen.gi_frame is None for gen in active)
 
     own = cent_ref[pl.ds(pl.multiple_of(doc * share, share), share), :].astype(F32)
     total = None
@@ -185,11 +237,12 @@
         pltpu.VMEM((local, nrows), F32),
         pltpu.VMEM((local, nrows), jnp.bfloat16),
         pltpu.VMEM((1, nrows), F32),
-        pltpu.VMEM((ncent, 1, nrows), F32),
+        pltpu.VMEM((ncent // 2, 1, nrows), F32),
+        pltpu.VMEM((2, 1, nrows), F32),
         pltpu.VMEM((local, LANES), F32),
         dma((nrows // 512,)),
-        dma((ncent,)),
-        dma((ncent,)),
+        dma((ncent // 2,)),
+        dma((ncent // 2,)),
     ]
     for b, (_, width, x_first) in enumerate(BLOCKS):
         w = width + (LANES if b == 0 else 0)

time: 58 us -> 52.6 us (0.907)
  the two profiles are of different devices: /device:TPU:2 before, /device:TPU:1 now
where the time goes in v3:
time: 52.6 us; the launch traced here: 52 us
  Pallas kernels  50.5 us (96%)
  local copies, waits for them, and re-layouts  1.47 us (3%)
    pallas_call x1, Pallas kernels, on_device(): pl.pallas_call(functools.partial(kernel, scale, ncent), out_shape=jax.Sha...  50.5 us
    unnamed x1, local copies, waits for them, and re-layouts  1.47 us

profile of v3, /device:TPU:1, one launch (start us, length us, event | category | flops | bytes accessed | tf_op | source)
XLA Modules:
  0.0 52.0 jit_solution(3963130419858105941)
XLA Ops:
  0.0 50.5 %shard_map.28 = f32[16,1024]{1,0:T(8,128)} custom-call(bf16[2048,1024]{1,0:T(8,128)(2,1)} %refs_0_.1, bf16[512,1024]{1,0:T(8,128)(2,1)} %refs_1_.1), custom_call_target="tpu_custom_call" | custom-call | tf_op jit(solution)/shard_map/pallas_call | solution.py:261
  50.6 1.5 %copy.4 = f32[16,1024]{1,0:T(8,128)} copy(f32[16,1024]{1,0:T(8,128)} %shard_map.28) | data formatting | bytes 131072

commit v4 on v3

--- a/solution.py
+++ b/solution.py
@@ -12,8 +12,8 @@
 F32 = jnp.float32
 NZ, NX = 8, 4
 LANES = 128
-BLOCKS = ((0, 128, True), (128, 256, False), (384, 256, True), (640, 128, True), (768, 256, False))
-ORDER = (1, 0, 4, 2, 3, 1, 4, 0, 1, 2, 4, 3, 0, 1, 2, 4, 3, 1, 0, 2, 4, 3)
+BLOCKS = ((0, 256, True), (256, 256, False), (512, 256, True), (768, 256, False))
+ORDER = (1, 0, 3, 2, 4, 1, 3, 0, 1, 2, 3, 0, 1, 2, 3, 1, 0, 2, 3, 4)
 
 
 def scatter(mode, me, n, device, data, half_in, full_in, send_sems, recv_sems, sent):
@@ -88,8 +88,9 @@
 
 def kernel(scale, ncent, *refs):
     rows_hbm, cent_ref, out_ref, x_v, p_v, resp_v, top_v, stat_v, pair_v, tot_v = refs[:10]
+    own_tot_v, x_tot_v, z_tot_v, x_send, x_recv, z_send, z_recv = refs[13:20]
     in_sems, stat_send, stat_recv = refs[10:13]
-    block_refs = [refs[13 + 9 * b : 22 + 9 * b] for b in range(len(BLOCKS))]
+    block_refs = [refs[20 + 9 * b : 29 + 9 * b] for b in range(len(BLOCKS))]
     rows, step = x_v.shape[0], 512
     nsteps = rows // step
     doc, cent = lax.axis_index("doc"), lax.axis_index("cent")
@@ -109,7 +110,7 @@
         return {"doc": z * NX + k}
 
     barrier = pltpu.get_barrier_semaphore()
-    near = [at_z(lax.rem(z + k, NZ)) for k in (1, 2, NZ - 2, NZ - 1)]
+    near = [at_z(lax.rem(z + k, NZ)) for k in range(1, NZ)]
     near += [at_x(lax.rem(x + k, NX)) for k in range(1, NX)]
     near += [{"cent": lax.rem(cent + k, ncent)} for k in range(2, ncent, 2)]
     partner = {"cent": cent + 1 - 2 * lax.rem(cent, 2)}
@@ -127,7 +128,8 @@
         p = jnp.exp(logits - top)
         p_v[:, part] = p
         top_v[:, part] = top
-        stat_v[0, :, part] = top + jnp.log(jnp.sum(p, axis=0, keepdims=True))
+        lse = top + jnp.log(jnp.sum(p, axis=0, keepdims=True))
+        stat_v[0, :, part] = lse
         return carry
 
     lax.fori_loop(0, nsteps, logits_step, 0)
@@ -194,6 +196,44 @@
         mode = "hub" if x_first else "direct"
         yield from scatter(mode, *second, data.at[first[0]], h2, f2, s2, r2, sent)
 
+    def run_totals():
+        for k in range(NX):
+            parts = [tot_v[pl.ds((j * NX + k) * share, share), :] for j in range(NZ)]
+            wide = jnp.concatenate(parts, axis=0)
+            own_tot_v[k] = jnp.sum(wide.T, axis=0, keepdims=True)
+        copies = []
+
+        def send(source, target, send_sem, recv_sem, device):
+            copies.append(
+                pltpu.make_async_remote_copy(
+                    src_ref=source,
+                    dst_ref=target,
+                    send_sem=send_sem,
+                    recv_sem=recv_sem,
+                    device_id=device,
+                    device_id_type=MESH,
+                )
+            )
+            copies[-1].start()
+            sent.append(copies[-1])
+
+        for k in range(1, NX):
+            to = lax.rem(x + k, NX)
+            send(own_tot_v.at[to], x_tot_v.at[k], x_send.at[k], x_recv.at[k], at_x(to))
+        yield
+        total = own_tot_v[x]
+        for k, copy in enumerate(copies):
+            copy.wait_recv()
+            total += x_tot_v[k + 1]
+        z_tot_v[0] = total
+        copies.clear()
+        for k in range(1, NZ):
+            to = lax.rem(z + k, NZ)
+            send(z_tot_v.at[0], z_tot_v.at[k], z_send.at[k], z_recv.at[k], at_z(to))
+        yield
+        for copy in copies:
+            copy.wait_recv()
+
     def put(data, x_first, first, width, value):
         for k in range(NZ):
             tile = value[k * NX * share : (k + 1) * NX * share].reshape(NX, share, width)
@@ -206,21 +246,22 @@
         data = block_refs[b][0]
         value = jnp.dot(resp_v[...], x_v[:, start : start + width], preferred_element_type=F32)
         put(data, x_first, 0, width, value)
-        if b == 0:
-            put(data, x_first, width, LANES, tot_v[...])
         active.append(run(b))
         next(active[-1])
+    active.append(run_totals())
+    next(active[-1])
     for b in ORDER:
         next(active[b], None)
     assert all(gen.gi_frame is None for gen in active)
 
     own = cent_ref[pl.ds(pl.multiple_of(doc * share, share), share), :].astype(F32)
-    total = None
+    row = jnp.sum(z_tot_v[...], axis=0)
+    lane = lax.broadcasted_iota(jnp.int32, (share, LANES), 1)
+    wanted = lax.broadcasted_iota(jnp.int32, (share, LANES), 0) + z * share
+    total = jnp.sum(jnp.where(lane == wanted, row, 0.0), axis=1, keepdims=True) + 1.0
     for b, (start, width, x_first) in enumerate(BLOCKS):
         value = block_refs[b][0][(x, z) if x_first else (z, x)]
-        if b == 0:
-            total = jnp.sum(value[:, width:], axis=1, keepdims=True) + 1.0
-        out_ref[:, start : start + width] = (value[:, :width] + own[:, start : start + width]) / total
+        out_ref[:, start : start + width] = (value + own[:, start : start + width]) / total
     for copy in stat_copies + sent:
         copy.wait_send()
 
@@ -230,6 +271,7 @@
     local = centroids.shape[0]
     ncent = lax.axis_size("cent")
     share = local // (NZ * NX)
+    assert share * NZ == LANES
     scale = 1.0 / (0.6 * math.sqrt(d))
     dma = pltpu.SemaphoreType.DMA
     scratch = [
@@ -243,9 +285,15 @@
         dma((nrows // 512,)),
         dma((ncent // 2,)),
         dma((ncent // 2,)),
+        pltpu.VMEM((NX, 1, LANES), F32),
+        pltpu.VMEM((NX, 1, LANES), F32),
+        pltpu.VMEM((NZ, 1, LANES), F32),
+        dma((NX,)),
+        dma((NX,)),
+        dma((NZ,)),
+        dma((NZ,)),
     ]
-    for b, (_, width, x_first) in enumerate(BLOCKS):
-        w = width + (LANES if b == 0 else 0)
+    for _, w, x_first in BLOCKS:
         n1, n2 = (NX, NZ) if x_first else (NZ, NX)
         scratch += [
             pltpu.VMEM((n1, n2, share, w), F32),

time: 52.6 us -> 51.5 us (0.979)
  Pallas kernels: 50.5 us -> 49.8 us
    pallas_call x1, Pallas kernels: 50.5 us -> 49.8 us  [on_device(): pl.pallas_call(functools.partial(kernel, scale, ncent), out_shape=jax.Sha...]
where the time goes in v4:
time: 51.5 us; the launch traced here: 51.3 us
  Pallas kernels  49.8 us (97%)
  local copies, waits for them, and re-layouts  1.47 us (3%)
    pallas_call x1, Pallas kernels, on_device(): pl.pallas_call(functools.partial(kernel, scale, ncent), out_shape=jax.Sha...  49.8 us
    unnamed x1, local copies, waits for them, and re-layouts  1.47 us

profile of v4, /device:TPU:1, one launch (start us, length us, event | category | flops | bytes accessed | tf_op | source)
XLA Modules:
  0.0 51.3 jit_solution(17944399089975355611)
XLA Ops:
  0.0 49.8 %shard_map.28 = f32[16,1024]{1,0:T(8,128)} custom-call(bf16[2048,1024]{1,0:T(8,128)(2,1)} %refs_0_.1, bf16[512,1024]{1,0:T(8,128)(2,1)} %refs_1_.1), custom_call_target="tpu_custom_call" | custom-call | tf_op jit(solution)/shard_map/pallas_call | solution.py:309
  49.8 1.5 %copy.4 = f32[16,1024]{1,0:T(8,128)} copy(f32[16,1024]{1,0:T(8,128)} %shard_map.28) | data formatting | bytes 131072

commit v5 on v4

--- a/solution.py
+++ b/solution.py
@@ -87,19 +87,21 @@
 
 
 def kernel(scale, ncent, *refs):
-    rows_hbm, cent_ref, out_ref, x_v, p_v, resp_v, top_v, stat_v, pair_v, tot_v = refs[:10]
-    own_tot_v, x_tot_v, z_tot_v, x_send, x_recv, z_send, z_recv = refs[13:20]
-    in_sems, stat_send, stat_recv = refs[10:13]
-    block_refs = [refs[20 + 9 * b : 29 + 9 * b] for b in range(len(BLOCKS))]
+    rows_hbm, cent_hbm, out_ref, cent_ref, x_v, p_v, resp_v, top_v, stat_v, pair_v, tot_v = refs[:11]
+    own_tot_v, x_tot_v, z_tot_v, x_send, x_recv, z_send, z_recv = refs[14:21]
+    in_sems, stat_send, stat_recv = refs[11:14]
+    block_refs = [refs[21 + 9 * b : 30 + 9 * b] for b in range(len(BLOCKS))]
     rows, step = x_v.shape[0], 512
     nsteps = rows // step
     doc, cent = lax.axis_index("doc"), lax.axis_index("cent")
     z, x = doc // NX, lax.rem(doc, NX)
 
     def chunk_in(i):
-        part = pl.ds(pl.multiple_of(i * step, step), step)
+        part = pl.ds(i * step, step)
         return pltpu.make_async_copy(rows_hbm.at[part], x_v.at[part], in_sems.at[i])
 
+    cent_in = pltpu.make_async_copy(cent_hbm, cent_ref, in_sems.at[nsteps])
+    cent_in.start()
     for i in range(nsteps):
         chunk_in(i).start()
 
@@ -118,21 +120,27 @@
     for other in near:
         pl.semaphore_signal(barrier, inc=1, device_id=other, device_id_type=MESH)
 
-    def logits_step(i, carry):
+    def logits_of(i):
         chunk_in(i).wait()
-        part = pl.ds(pl.multiple_of(i * step, step), step)
-        logits = lax.dot_general(
-            cent_ref[...], x_v[part, :], (((1,), (1,)), ((), ())), preferred_element_type=F32
-        ) * scale
+        return lax.dot_general(
+            cent_ref[...],
+            x_v[i * step : (i + 1) * step, :],
+            (((1,), (1,)), ((), ())),
+            preferred_element_type=F32,
+        )
+
+    cent_in.wait()
+    product = logits_of(0)
+    for i in range(nsteps):
+        following = logits_of(i + 1) if i + 1 < nsteps else None
+        part = slice(i * step, (i + 1) * step)
+        logits = product * scale
         top = jnp.max(logits, axis=0, keepdims=True)
         p = jnp.exp(logits - top)
         p_v[:, part] = p
         top_v[:, part] = top
-        lse = top + jnp.log(jnp.sum(p, axis=0, keepdims=True))
-        stat_v[0, :, part] = lse
-        return carry
-
-    lax.fori_loop(0, nsteps, logits_step, 0)
+        stat_v[0, :, part] = top + jnp.log(jnp.sum(p, axis=0, keepdims=True))
+        product = following
     pl.semaphore_wait(barrier, len(near))
 
     def log_sum_exp(values):
@@ -168,20 +176,15 @@
     stat_copies.append(swap)
     swap.wait_recv()
     top_v[...] = jnp.exp(top_v[...] - log_sum_exp(pair_v[...]))
-    tot_v[...] = jnp.zeros_like(tot_v)
-
-    def resp_step(i, carry):
-        part = pl.ds(pl.multiple_of(i * step, step), step)
+    total = jnp.zeros(tot_v.shape, F32)
+    for i in range(nsteps):
+        part = slice(i * step, (i + 1) * step)
         resp = (p_v[:, part] * top_v[:, part]).astype(jnp.bfloat16)
         resp_v[:, part] = resp
         wide = resp.astype(F32)
-        total = tot_v[...]
         for j in range(step // LANES):
             total += wide[:, j * LANES : (j + 1) * LANES]
-        tot_v[...] = total
-        return carry
-
-    lax.fori_loop(0, nsteps, resp_step, 0)
+    tot_v[...] = total
 
     sent = []
     active = []
@@ -275,6 +278,7 @@
     scale = 1.0 / (0.6 * math.sqrt(d))
     dma = pltpu.SemaphoreType.DMA
     scratch = [
+        pltpu.VMEM((local, d), jnp.bfloat16),
         pltpu.VMEM((nrows, d), jnp.bfloat16),
         pltpu.VMEM((local, nrows), F32),
         pltpu.VMEM((local, nrows), jnp.bfloat16),
@@ -282,7 +286,7 @@
         pltpu.VMEM((ncent // 2, 1, nrows), F32),
         pltpu.VMEM((2, 1, nrows), F32),
         pltpu.VMEM((local, LANES), F32),
-        dma((nrows // 512,)),
+        dma((nrows // 512 + 1,)),
         dma((ncent // 2,)),
         dma((ncent // 2,)),
         pltpu.VMEM((NX, 1, LANES), F32),
@@ -309,7 +313,7 @@
     return pl.pallas_call(
         functools.partial(kernel, scale, ncent),
         out_shape=jax.ShapeDtypeStruct((share, d), F32),
-        in_specs=[pl.BlockSpec(memory_space=pl.ANY), pl.BlockSpec(memory_space=pltpu.VMEM)],
+        in_specs=[pl.BlockSpec(memory_space=pl.ANY)] * 2,
         out_specs=pl.BlockSpec(memory_space=pltpu.VMEM),
         scratch_shapes=scratch,
         compiler_params=pltpu.CompilerParams(collective_id=0, has_side_effects=True),

time: 51.5 us -> 49.6 us (0.963)
  Pallas kernels: 49.8 us -> 48 us
    pallas_call x1, Pallas kernels: 49.8 us -> 48 us  [on_device(): pl.pallas_call(functools.partial(kernel, scale, ncent), out_shape=jax.Sha...]
where the time goes in v5:
time: 49.6 us; the launch traced here: 49.5 us
  Pallas kernels  48 us (97%)
  local copies, waits for them, and re-layouts  1.47 us (3%)
    pallas_call x1, Pallas kernels, on_device(): pl.pallas_call(functools.partial(kernel, scale, ncent), out_shape=jax.Sha...  48 us
    unnamed x1, local copies, waits for them, and re-layouts  1.47 us

profile of v5, /device:TPU:1, one launch (start us, length us, event | category | flops | bytes accessed | tf_op | source)
XLA Modules:
  0.0 49.5 jit_solution(17314076904877432255)
XLA Ops:
  0.0 48.0 %shard_map.28 = f32[16,1024]{1,0:T(8,128)} custom-call(bf16[2048,1024]{1,0:T(8,128)(2,1)} %refs_0_.1, bf16[512,1024]{1,0:T(8,128)(2,1)} %refs_1_.1), custom_call_target="tpu_custom_call" | custom-call | tf_op jit(solution)/shard_map/pallas_call | solution.py:313
  48.0 1.5 %copy.4 = f32[16,1024]{1,0:T(8,128)} copy(f32[16,1024]{1,0:T(8,128)} %shard_map.28) | data formatting | bytes 131072
